TPU v7x, 256 devices: a whole 4x4x8 slice. The times are simulated.
256 devices in a mesh: section: 8 (over z), lon: 32 (over y, x, core).
Axes of the slice: x: 4, y: 4, z: 8, core: 2. Of those that a mesh axis runs over, the one named last changes fastest.
Arguments:
- lanczos_block: bfloat16 [16, 8, 256, 512], P(None, None, 'lon'), may hold values from -9 to 9
- previous: bfloat16 [16, 8, 256, 512], P(None, 'section', 'lon'), may hold values from -6 to 6
- beta_prev: float32 [16, 16], replicated, may hold values from -2 to 2, as said below
- weights: bfloat16 [8, 9, 512, 512], P('section'), may hold values from -0.09375 to 0.09375
- act_slope: bfloat16 [8, 8, 256, 512], P('section', None, 'lon'), may hold values from 0 to 1.09375
- metric: float32 [8, 256], P(None, 'lon'), may hold values from 0.3 to 3
Outputs:
- residual_block: float32 [16, 8, 256, 512], P(None, 'section', 'lon')
- projection: float32 [16, 16], replicated
- residual_gram: float32 [16, 16], replicated
Inputs may be any that keep to these rules, and one draw needn't show every extreme that they name: `beta_prev`: upper triangular, with a positive diagonal.
All inputs are finite; a program needn't handle non-finite values.
Results may differ from a plain program's by a relative error of at most 0.02.
Values may be sent and summed in bfloat16 or wider, within the bound.
No kernel may reach another device: no remote copies, remote signals or barrier semaphores. Data moves between devices by JAX's collectives and lax.ppermute only.
A program may use at most 64 MiB of HBM per device.

v0:
```python
import jax
import jax.numpy as jnp
from jax import lax
from jax.sharding import PartitionSpec as P

K = 16
DILATION_SIZE = 4


def padded(cells, sides, width):
    for axis, dim in sides:
        count = lax.axis_size(axis)
        head = lax.slice_in_dim(cells, 0, width, axis=dim)
        tail = lax.slice_in_dim(cells, cells.shape[dim] - width, cells.shape[dim], axis=dim)
        cells = jnp.concatenate(
            [
                lax.ppermute(tail, axis, [(i, (i + 1) % count) for i in range(count)]),
                cells,
                lax.ppermute(head, axis, [((i + 1) % count, i) for i in range(count)]),
            ],
            axis=dim,
        )
    return cells


def from_behind(shard, axis, by):
    count = lax.axis_size(axis)
    pairs = [(i, i + by) for i in range(count) if 0 <= i + by < count]
    return lax.ppermute(shard, axis, pairs)


def broadcast(shard, axis, root):
    mine = lax.axis_index(axis) == root
    return lax.psum(jnp.where(mine, shard, jnp.zeros_like(shard)), axis)


def spread_taps(input_field, tap_weights, direction_sign, border_width):
    micro_size = input_field.shape[0]
    lat_rows = input_field.shape[1]
    lon_cols = input_field.shape[2] - 2 * border_width
    channels = input_field.shape[3]
    padded_field = jnp.pad(input_field, ((0, 0), (border_width, border_width), (0, 0), (0, 0)))
    summed = jnp.zeros((micro_size * lat_rows * lon_cols, channels), jnp.float32)
    for row_stride in (-1, 0, 1):
        for column_stride in (-1, 0, 1):
            tap_index = 3 * (row_stride + 1) + (column_stride + 1)
            first_row = border_width + direction_sign * row_stride * border_width
            col_start = border_width + direction_sign * column_stride * border_width
            tap_rows = padded_field[
                :, first_row : first_row + lat_rows, col_start : col_start + lon_cols, :
            ].reshape(-1, channels)
            if direction_sign > 0:
                summed = summed + jnp.dot(
                    tap_rows, tap_weights[tap_index], preferred_element_type=jnp.float32
                )
            else:
                summed = summed + lax.dot_general(
                    tap_rows,
                    tap_weights[tap_index],
                    (((1,), (1,)), ((), ())),
                    preferred_element_type=jnp.float32,
                )
    return summed.reshape(micro_size, lat_rows, lon_cols, channels)


def body(lanczos_block, previous, beta_prev, weights, act_slope, metric):
    section_count = lax.axis_size("section")
    section_index = lax.axis_index("section")
    tap_weights = weights[0]
    slope_here = act_slope[0].astype(jnp.float32)[None]
    border_width = DILATION_SIZE
    micro_count = 2
    micro_size = K // micro_count
    slot_shape = (micro_size,) + lanczos_block.shape[1:]
    lon_cols = lanczos_block.shape[2]
    micro_feeds = lanczos_block.reshape((micro_count,) + slot_shape)
    tick_count = micro_count + section_count - 1
    zero_slot = jnp.zeros(slot_shape, jnp.bfloat16)
    empty_store = jnp.zeros((micro_count,) + slot_shape, jnp.bfloat16)

    def forward_layer(rimmed):
        convolved = spread_taps(rimmed, tap_weights, 1, border_width)
        centre = rimmed[:, :, border_width : border_width + lon_cols, :].astype(jnp.float32)
        return (centre + slope_here * convolved).astype(jnp.bfloat16)

    def skip_forward(rimmed):
        return zero_slot

    def forward_tick(state_pair, tick_now):
        inbound, forward_out = state_pair
        micro_index = tick_now - section_index
        active = (micro_index >= 0) & (micro_index < micro_count)
        slot_index = jnp.clip(micro_index, 0, micro_count - 1)
        fed_slot = lax.dynamic_index_in_dim(micro_feeds, slot_index, 0, keepdims=False)
        incoming = jnp.where(section_index == 0, fed_slot, inbound)
        rimmed = padded(incoming, (("lon", 2),), border_width)
        result = lax.cond(active, forward_layer, skip_forward, rimmed)
        keep_slot = active & (section_index == section_count - 1)
        old_slot = lax.dynamic_index_in_dim(forward_out, slot_index, 0, keepdims=False)
        forward_out = lax.dynamic_update_index_in_dim(
            forward_out, jnp.where(keep_slot, result, old_slot), slot_index, 0
        )
        outbound = from_behind(result, "section", 1)
        return ((outbound, forward_out), None)

    (unused_slot, forward_out), unused_out = lax.scan(
        forward_tick, (zero_slot, empty_store), jnp.arange(tick_count, dtype=jnp.int32)
    )
    metric_here = metric[None, :, :, None]

    def backward_layer(operands):
        incoming, rimmed = operands
        convolved = spread_taps(rimmed, tap_weights, -1, border_width)
        return (incoming.astype(jnp.float32) + convolved).astype(jnp.bfloat16)

    def skip_backward(operands):
        return zero_slot

    def backward_tick(state_pair, tick_now):
        inbound, adjoint_out = state_pair
        micro_index = tick_now - (section_count - 1 - section_index)
        active = (micro_index >= 0) & (micro_index < micro_count)
        slot_index = jnp.clip(micro_index, 0, micro_count - 1)
        stored_slot = lax.dynamic_index_in_dim(forward_out, slot_index, 0, keepdims=False)
        started = (metric_here * stored_slot.astype(jnp.float32)).astype(jnp.bfloat16)
        incoming = jnp.where(section_index == section_count - 1, started, inbound)
        sensitivity = (slope_here * incoming.astype(jnp.float32)).astype(jnp.bfloat16)
        rimmed = padded(sensitivity, (("lon", 2),), border_width)
        result = lax.cond(active, backward_layer, skip_backward, (incoming, rimmed))
        keep_slot = active & (section_index == 0)
        old_slot = lax.dynamic_index_in_dim(adjoint_out, slot_index, 0, keepdims=False)
        adjoint_out = lax.dynamic_update_index_in_dim(
            adjoint_out, jnp.where(keep_slot, result, old_slot), slot_index, 0
        )
        outbound = from_behind(result, "section", -1)
        return ((outbound, adjoint_out), None)

    (unused_back, adjoint_out), unused_more = lax.scan(
        backward_tick, (zero_slot, empty_store), jnp.arange(tick_count, dtype=jnp.int32)
    )
    applied = adjoint_out.reshape(lanczos_block.shape)
    applied_all = broadcast(applied, "section", 0)
    row_count = previous.shape[1]
    applied_rows = lax.dynamic_slice_in_dim(applied_all, section_index * row_count, row_count, 1)
    own_block = lax.dynamic_slice_in_dim(lanczos_block, section_index * row_count, row_count, 1)
    high = lax.Precision.HIGHEST
    cell_count = (
        lanczos_block.shape[1]
        * lanczos_block.shape[2]
        * lax.axis_size("lon")
        * lanczos_block.shape[3]
    )
    block_flat = own_block.reshape(K, -1).astype(jnp.float32)
    prev_flat = previous.reshape(K, -1).astype(jnp.float32)
    shifted = applied_rows.reshape(K, -1).astype(jnp.float32) - jnp.dot(
        beta_prev, prev_flat, precision=high
    )
    part_projection = jnp.dot(block_flat, shifted.T, precision=high) / cell_count
    projection = lax.psum(part_projection, ("section", "lon"))
    residual_rows = shifted - jnp.dot(projection.T, block_flat, precision=high)
    part_gram = jnp.dot(residual_rows, residual_rows.T, precision=high) / cell_count
    residual_gram = lax.psum(part_gram, ("section", "lon"))
    return (residual_rows.reshape(own_block.shape), projection, residual_gram)


def solution(mesh):
    return jax.shard_map(
        body,
        mesh=mesh,
        in_specs=(
            P(None, None, "lon", None),
            P(None, "section", "lon", None),
            P(),
            P("section", None, None, None),
            P("section", None, "lon", None),
            P(None, "lon"),
        ),
        out_specs=(P(None, "section", "lon", None), P(), P()),
        check_vma=False,
    )
```

profile of v0, /device:TPU:1, one launch (start us, length us, event | category | flops | bytes accessed | tf_op | source)
XLA Modules:
  0.0 797.1 jit_solution(21797135074578725)
XLA Ops:
  8.3 248.3 %while.27 = (s32[]{:T(128)}, bf16[8,8,8,512]{3,2,1,0:T(8,128)(2,1)S(1)}, bf16[2,8,8,8,512]{4,3,2,1,0:T(8,128)(2,1)S(1)}, s32[9]{0:T(128)S(1)}, s32[]{:T(128)}, /...) while((s32[]{:T(128)}, ...), condition=%wide.region_3.4_spmd, body=%wide.region_0.3_spmd.sunk | while | flops 2422734848 | bytes 67240344 | solution.py:106
  18.7 6.5 conditional.4
  26.8 5.8 collective-permute-done.2
  35.1 8.7 %collective-permute-start = (bf16[8,8,4,512]{3,2,1,0:T(4,128)(2,1)S(1)}, bf16[8,8,4,512]{3,2,1,0:T(4,128)(2,1)S(1)}, u32[]{:S(2)}, u32[]{:S(2)}) collective-permute-start(bf16[8,8,4,512]{3,2,1,0:T(4,128)(2,1)S(1)} %get-tuple-element.424), channel_id=1, source_target_pairs={{1,0},{2,1},{3,2},{4,3},{5,4},{6,5},{7,6},{8,7},{9,8},{10,9},{11,1... | collective-permute-start | bytes 786440 | tf_op jit(solution)/shard_map/while/body/eval_jaxpr/ppermute | solution.py:19
  48.4 6.5 conditional.4
  59.0 5.8 collective-permute-done.2
  67.3 9.0 %collective-permute-start = (bf16[8,8,4,512]{3,2,1,0:T(4,128)(2,1)S(1)}, bf16[8,8,4,512]{3,2,1,0:T(4,128)(2,1)S(1)}, u32[]{:S(2)}, u32[]{:S(2)}) collective-permute-start(bf16[8,8,4,512]{3,2,1,0:T(4,128)(2,1)S(1)} %get-tuple-element.424), channel_id=1, source_target_pairs={{1,0},{2,1},{3,2},{4,3},{5,4},{6,5},{7,6},{8,7},{9,8},{10,9},{11,1... | collective-permute-start | bytes 786440 | tf_op jit(solution)/shard_map/while/body/eval_jaxpr/ppermute | solution.py:19
  80.4 10.6 %collective-permute-start.2 = (bf16[8,8,8,512]{3,2,1,0:T(8,128)(2,1)S(1)}, bf16[8,8,8,512]{3,2,1,0:T(8,128)(2,1)S(1)}, u32[]{:S(2)}, u32[]{:S(2)}) collective-permute-start(bf16[8,8,8,512]{3,2,1,0:T(8,128)(2,1)S(1)} %get-tuple-element.522), channel_id=1, source_target_pairs={{0,32},{32,64},{64,96},{96,128},{128,160},{160,192},{192,224},{1,3... | collective-permute-start | bytes 1572872 | tf_op jit(solution)/shard_map/while/body/eval_jaxpr/ppermute | solution.py:29
  91.2 5.8 collective-permute-done.2
  99.6 8.1 %collective-permute-start = (bf16[8,8,4,512]{3,2,1,0:T(4,128)(2,1)S(1)}, bf16[8,8,4,512]{3,2,1,0:T(4,128)(2,1)S(1)}, u32[]{:S(2)}, u32[]{:S(2)}) collective-permute-start(bf16[8,8,4,512]{3,2,1,0:T(4,128)(2,1)S(1)} %get-tuple-element.424), channel_id=1, source_target_pairs={{1,0},{2,1},{3,2},{4,3},{5,4},{6,5},{7,6},{8,7},{9,8},{10,9},{11,1... | collective-permute-start | bytes 786440 | tf_op jit(solution)/shard_map/while/body/eval_jaxpr/ppermute | solution.py:19
  116.1 5.8 collective-permute-done.2
  124.4 7.2 collective-permute-start
  135.7 8.7 %collective-permute-start.2 = (bf16[8,8,8,512]{3,2,1,0:T(8,128)(2,1)S(1)}, bf16[8,8,8,512]{3,2,1,0:T(8,128)(2,1)S(1)}, u32[]{:S(2)}, u32[]{:S(2)}) collective-permute-start(bf16[8,8,8,512]{3,2,1,0:T(8,128)(2,1)S(1)} %get-tuple-element.522), channel_id=1, source_target_pairs={{0,32},{32,64},{64,96},{96,128},{128,160},{160,192},{192,224},{1,3... | collective-permute-start | bytes 1572872 | tf_op jit(solution)/shard_map/while/body/eval_jaxpr/ppermute | solution.py:29
  144.6 5.8 collective-permute-done.2
  152.9 7.4 collective-permute-start
  168.8 5.8 collective-permute-done.2
  177.1 6.8 collective-permute-start
  188.0 8.7 %collective-permute-start.2 = (bf16[8,8,8,512]{3,2,1,0:T(8,128)(2,1)S(1)}, bf16[8,8,8,512]{3,2,1,0:T(8,128)(2,1)S(1)}, u32[]{:S(2)}, u32[]{:S(2)}) collective-permute-start(bf16[8,8,8,512]{3,2,1,0:T(8,128)(2,1)S(1)} %get-tuple-element.522), channel_id=1, source_target_pairs={{0,32},{32,64},{64,96},{96,128},{128,160},{160,192},{192,224},{1,3... | collective-permute-start | bytes 1572872 | tf_op jit(solution)/shard_map/while/body/eval_jaxpr/ppermute | solution.py:29
  196.9 5.8 collective-permute-done.2
  205.2 6.8 collective-permute-start
  220.5 5.8 collective-permute-done.2
  228.8 6.8 collective-permute-start
  239.7 10.7 %collective-permute-start.2 = (bf16[8,8,8,512]{3,2,1,0:T(8,128)(2,1)S(1)}, bf16[8,8,8,512]{3,2,1,0:T(8,128)(2,1)S(1)}, u32[]{:S(2)}, u32[]{:S(2)}) collective-permute-start(bf16[8,8,8,512]{3,2,1,0:T(8,128)(2,1)S(1)} %get-tuple-element.522), channel_id=1, source_target_pairs={{0,32},{32,64},{64,96},{96,128},{128,160},{160,192},{192,224},{1,3... | collective-permute-start | bytes 1572872 | tf_op jit(solution)/shard_map/while/body/eval_jaxpr/ppermute | solution.py:29
  250.7 5.8 collective-permute-done.2
  257.5 306.7 %while.28 = (s32[]{:T(128)}, bf16[8,8,8,512]{3,2,1,0:T(8,128)(2,1)}, bf16[2,8,8,8,512]{4,3,2,1,0:T(8,128)(2,1)S(1)}, s32[9]{0:T(128)S(1)}, s32[]{:T(128)}, /*ind...) while((s32[]{:T(128)}, ...), condition=%wide.region_7.8_spmd, body=%wide.region_4.7_spmd.sunk | while | flops 2424045568 | bytes 67764888 | solution.py:138
  261.0 6.7 collective-permute-start.3
  274.4 10.3 %collective-permute-done.5 = bf16[8,8,8,512]{3,2,1,0:T(8,128)(2,1)} collective-permute-done((bf16[8,8,8,512]{3,2,1,0:T(8,128)(2,1)S(1)}, bf16[8,8,8,512]{3,2,1,0:T(8,128)(2,1)}, u32[]{:S(2)}, u32[]{:S(2)}) %collective-permute-start.5) | collective-permute-done | bytes 524320 | tf_op jit(solution)/shard_map/while/body/eval_jaxpr/ppermute | solution.py:29
  288.2 6.8 collective-permute-start.3
  301.6 12.0 %collective-permute-done.5 = bf16[8,8,8,512]{3,2,1,0:T(8,128)(2,1)} collective-permute-done((bf16[8,8,8,512]{3,2,1,0:T(8,128)(2,1)S(1)}, bf16[8,8,8,512]{3,2,1,0:T(8,128)(2,1)}, u32[]{:S(2)}, u32[]{:S(2)}) %collective-permute-start.5) | collective-permute-done | bytes 524320 | tf_op jit(solution)/shard_map/while/body/eval_jaxpr/ppermute | solution.py:29
  317.2 6.8 collective-permute-start.3
  330.6 10.5 %collective-permute-done.5 = bf16[8,8,8,512]{3,2,1,0:T(8,128)(2,1)} collective-permute-done((bf16[8,8,8,512]{3,2,1,0:T(8,128)(2,1)S(1)}, bf16[8,8,8,512]{3,2,1,0:T(8,128)(2,1)}, u32[]{:S(2)}, u32[]{:S(2)}) %collective-permute-start.5) | collective-permute-done | bytes 524320 | tf_op jit(solution)/shard_map/while/body/eval_jaxpr/ppermute | solution.py:29
  344.6 6.8 collective-permute-start.3
  358.0 12.0 %collective-permute-done.5 = bf16[8,8,8,512]{3,2,1,0:T(8,128)(2,1)} collective-permute-done((bf16[8,8,8,512]{3,2,1,0:T(8,128)(2,1)S(1)}, bf16[8,8,8,512]{3,2,1,0:T(8,128)(2,1)}, u32[]{:S(2)}, u32[]{:S(2)}) %collective-permute-start.5) | collective-permute-done | bytes 524320 | tf_op jit(solution)/shard_map/while/body/eval_jaxpr/ppermute | solution.py:29
  373.6 6.8 collective-permute-start.3
  386.9 10.0 %collective-permute-done.5 = bf16[8,8,8,512]{3,2,1,0:T(8,128)(2,1)} collective-permute-done((bf16[8,8,8,512]{3,2,1,0:T(8,128)(2,1)S(1)}, bf16[8,8,8,512]{3,2,1,0:T(8,128)(2,1)}, u32[]{:S(2)}, u32[]{:S(2)}) %collective-permute-start.5) | collective-permute-done | bytes 524320 | tf_op jit(solution)/shard_map/while/body/eval_jaxpr/ppermute | solution.py:29
  400.5 6.8 collective-permute-start.3
  413.9 12.5 %collective-permute-done.5 = bf16[8,8,8,512]{3,2,1,0:T(8,128)(2,1)} collective-permute-done((bf16[8,8,8,512]{3,2,1,0:T(8,128)(2,1)S(1)}, bf16[8,8,8,512]{3,2,1,0:T(8,128)(2,1)}, u32[]{:S(2)}, u32[]{:S(2)}) %collective-permute-start.5) | collective-permute-done | bytes 524320 | tf_op jit(solution)/shard_map/while/body/eval_jaxpr/ppermute | solution.py:29
  429.9 6.8 collective-permute-start.3
  443.3 54.9 %collective-permute-done.5 = bf16[8,8,8,512]{3,2,1,0:T(8,128)(2,1)} collective-permute-done((bf16[8,8,8,512]{3,2,1,0:T(8,128)(2,1)S(1)}, bf16[8,8,8,512]{3,2,1,0:T(8,128)(2,1)}, u32[]{:S(2)}, u32[]{:S(2)}) %collective-permute-start.5) | collective-permute-done | bytes 524320 | tf_op jit(solution)/shard_map/while/body/eval_jaxpr/ppermute | solution.py:29
  501.8 6.8 collective-permute-start.3
  513.6 6.8 conditional.5
  522.0 10.0 %collective-permute-done.5 = bf16[8,8,8,512]{3,2,1,0:T(8,128)(2,1)} collective-permute-done((bf16[8,8,8,512]{3,2,1,0:T(8,128)(2,1)S(1)}, bf16[8,8,8,512]{3,2,1,0:T(8,128)(2,1)}, u32[]{:S(2)}, u32[]{:S(2)}) %collective-permute-start.5) | collective-permute-done | bytes 524320 | tf_op jit(solution)/shard_map/while/body/eval_jaxpr/ppermute | solution.py:29
  535.5 6.8 collective-permute-start.3
  547.3 6.8 conditional.5
  555.7 8.5 %collective-permute-done.5 = bf16[8,8,8,512]{3,2,1,0:T(8,128)(2,1)} collective-permute-done((bf16[8,8,8,512]{3,2,1,0:T(8,128)(2,1)S(1)}, bf16[8,8,8,512]{3,2,1,0:T(8,128)(2,1)}, u32[]{:S(2)}, u32[]{:S(2)}) %collective-permute-start.5) | collective-permute-done | bytes 524320 | tf_op jit(solution)/shard_map/while/body/eval_jaxpr/ppermute | solution.py:29
  566.4 67.9 %all-reduce.4.cloned.1.call-done = bf16[16,8,8,512]{3,2,0,1:T(8,128)(2,1)} async-done(((bf16[16,8,8,512]{3,2,0,1:T(8,128)(2,1)}), bf16[16,8,8,512]{3,2,0,1:T(8,128)(2,1)}) %all-reduce.4.cloned.1.call-update) | async-done | bytes 1048592 | tf_op jit(solution)/shard_map/psum | solution.py:34
  636.0 79.2 %psum.22 = f32[16,16]{1,0:T(8,128)S(1)} all-reduce(f32[16,16]{1,0:T(8,128)S(1)} %convolution_multiply_fusion.1), channel_id=1, replica_groups=mesh['section'=8,'lon'=32] {'section','lon'}, use_global_device_ids=true, to_apply=%region_9.10 | all-reduce | flops 256 | bytes 2048 | tf_op jit(solution)/shard_map/psum | solution.py:159
  716.9 73.3 %psum.23 = f32[16,16]{1,0:T(8,128)} all-reduce(f32[16,16]{1,0:T(8,128)S(1)} %convolution_multiply_fusion), channel_id=1, replica_groups=mesh['section'=8,'lon'=32] {'section','lon'}, use_global_device_ids=true, to_apply=%region_10.11 | all-reduce | flops 256 | bytes 2048 | tf_op jit(solution)/shard_map/psum | solution.py:162
  (286 shorter events, 196.7 us)
Async XLA Ops:
  7.2 627.2 %all-reduce.4.cloned.1.call-start = ((), (), s32[]{:S(2)}) async-start(), calls=%async_computation | async-start | bytes 2097152 | tf_op jit(solution)/shard_map/psum | solution.py:34
  10.8 6.7 collective-permute-start
  14.0 4.0 collective-permute-start.1
  25.2 7.4 collective-permute-start.2
  35.1 11.0 %collective-permute-start = (bf16[8,8,4,512]{3,2,1,0:T(4,128)(2,1)S(1)}, bf16[8,8,4,512]{3,2,1,0:T(4,128)(2,1)S(1)}, u32[]{:S(2)}, u32[]{:S(2)}) collective-permute-start(bf16[8,8,4,512]{3,2,1,0:T(4,128)(2,1)S(1)} %get-tuple-element.424), channel_id=1, source_target_pairs={{1,0},{2,1},{3,2},{4,3},{5,4},{6,5},{7,6},{8,7},{9,8},{10,9},{11,1... | collective-permute-start | bytes 786440 | tf_op jit(solution)/shard_map/while/body/eval_jaxpr/ppermute | solution.py:19
  43.8 3.9 collective-permute-start.1
  54.9 9.9 %collective-permute-start.2 = (bf16[8,8,8,512]{3,2,1,0:T(8,128)(2,1)S(1)}, bf16[8,8,8,512]{3,2,1,0:T(8,128)(2,1)S(1)}, u32[]{:S(2)}, u32[]{:S(2)}) collective-permute-start(bf16[8,8,8,512]{3,2,1,0:T(8,128)(2,1)S(1)} %get-tuple-element.522), channel_id=1, source_target_pairs={{0,32},{32,64},{64,96},{96,128},{128,160},{160,192},{192,224},{1,3... | collective-permute-start | bytes 1572872 | tf_op jit(solution)/shard_map/while/body/eval_jaxpr/ppermute | solution.py:29
  67.3 10.2 %collective-permute-start = (bf16[8,8,4,512]{3,2,1,0:T(4,128)(2,1)S(1)}, bf16[8,8,4,512]{3,2,1,0:T(4,128)(2,1)S(1)}, u32[]{:S(2)}, u32[]{:S(2)}) collective-permute-start(bf16[8,8,4,512]{3,2,1,0:T(4,128)(2,1)S(1)} %get-tuple-element.424), channel_id=1, source_target_pairs={{1,0},{2,1},{3,2},{4,3},{5,4},{6,5},{7,6},{8,7},{9,8},{10,9},{11,1... | collective-permute-start | bytes 786440 | tf_op jit(solution)/shard_map/while/body/eval_jaxpr/ppermute | solution.py:19
  76.3 3.3 collective-permute-start.1
  80.4 16.7 %collective-permute-start.2 = (bf16[8,8,8,512]{3,2,1,0:T(8,128)(2,1)S(1)}, bf16[8,8,8,512]{3,2,1,0:T(8,128)(2,1)S(1)}, u32[]{:S(2)}, u32[]{:S(2)}) collective-permute-start(bf16[8,8,8,512]{3,2,1,0:T(8,128)(2,1)S(1)} %get-tuple-element.522), channel_id=1, source_target_pairs={{0,32},{32,64},{64,96},{96,128},{128,160},{160,192},{192,224},{1,3... | collective-permute-start | bytes 1572872 | tf_op jit(solution)/shard_map/while/body/eval_jaxpr/ppermute | solution.py:29
  99.6 9.3 %collective-permute-start = (bf16[8,8,4,512]{3,2,1,0:T(4,128)(2,1)S(1)}, bf16[8,8,4,512]{3,2,1,0:T(4,128)(2,1)S(1)}, u32[]{:S(2)}, u32[]{:S(2)}) collective-permute-start(bf16[8,8,4,512]{3,2,1,0:T(4,128)(2,1)S(1)} %get-tuple-element.424), channel_id=1, source_target_pairs={{1,0},{2,1},{3,2},{4,3},{5,4},{6,5},{7,6},{8,7},{9,8},{10,9},{11,1... | collective-permute-start | bytes 786440 | tf_op jit(solution)/shard_map/while/body/eval_jaxpr/ppermute | solution.py:19
  107.7 3.3 collective-permute-start.1
  111.7 10.2 %collective-permute-start.2 = (bf16[8,8,8,512]{3,2,1,0:T(8,128)(2,1)S(1)}, bf16[8,8,8,512]{3,2,1,0:T(8,128)(2,1)S(1)}, u32[]{:S(2)}, u32[]{:S(2)}) collective-permute-start(bf16[8,8,8,512]{3,2,1,0:T(8,128)(2,1)S(1)} %get-tuple-element.522), channel_id=1, source_target_pairs={{0,32},{32,64},{64,96},{96,128},{128,160},{160,192},{192,224},{1,3... | collective-permute-start | bytes 1572872 | tf_op jit(solution)/shard_map/while/body/eval_jaxpr/ppermute | solution.py:29
  124.4 8.3 %collective-permute-start = (bf16[8,8,4,512]{3,2,1,0:T(4,128)(2,1)S(1)}, bf16[8,8,4,512]{3,2,1,0:T(4,128)(2,1)S(1)}, u32[]{:S(2)}, u32[]{:S(2)}) collective-permute-start(bf16[8,8,4,512]{3,2,1,0:T(4,128)(2,1)S(1)} %get-tuple-element.424), channel_id=1, source_target_pairs={{1,0},{2,1},{3,2},{4,3},{5,4},{6,5},{7,6},{8,7},{9,8},{10,9},{11,1... | collective-permute-start | bytes 786440 | tf_op jit(solution)/shard_map/while/body/eval_jaxpr/ppermute | solution.py:19
  131.6 3.3 collective-permute-start.1
  135.7 14.8 %collective-permute-start.2 = (bf16[8,8,8,512]{3,2,1,0:T(8,128)(2,1)S(1)}, bf16[8,8,8,512]{3,2,1,0:T(8,128)(2,1)S(1)}, u32[]{:S(2)}, u32[]{:S(2)}) collective-permute-start(bf16[8,8,8,512]{3,2,1,0:T(8,128)(2,1)S(1)} %get-tuple-element.522), channel_id=1, source_target_pairs={{0,32},{32,64},{64,96},{96,128},{128,160},{160,192},{192,224},{1,3... | collective-permute-start | bytes 1572872 | tf_op jit(solution)/shard_map/while/body/eval_jaxpr/ppermute | solution.py:29
  152.9 8.6 %collective-permute-start = (bf16[8,8,4,512]{3,2,1,0:T(4,128)(2,1)S(1)}, bf16[8,8,4,512]{3,2,1,0:T(4,128)(2,1)S(1)}, u32[]{:S(2)}, u32[]{:S(2)}) collective-permute-start(bf16[8,8,4,512]{3,2,1,0:T(4,128)(2,1)S(1)} %get-tuple-element.424), channel_id=1, source_target_pairs={{1,0},{2,1},{3,2},{4,3},{5,4},{6,5},{7,6},{8,7},{9,8},{10,9},{11,1... | collective-permute-start | bytes 786440 | tf_op jit(solution)/shard_map/while/body/eval_jaxpr/ppermute | solution.py:19
  160.3 3.3 collective-permute-start.1
  164.4 10.2 %collective-permute-start.2 = (bf16[8,8,8,512]{3,2,1,0:T(8,128)(2,1)S(1)}, bf16[8,8,8,512]{3,2,1,0:T(8,128)(2,1)S(1)}, u32[]{:S(2)}, u32[]{:S(2)}) collective-permute-start(bf16[8,8,8,512]{3,2,1,0:T(8,128)(2,1)S(1)} %get-tuple-element.522), channel_id=1, source_target_pairs={{0,32},{32,64},{64,96},{96,128},{128,160},{160,192},{192,224},{1,3... | collective-permute-start | bytes 1572872 | tf_op jit(solution)/shard_map/while/body/eval_jaxpr/ppermute | solution.py:29
  177.1 8.0 %collective-permute-start = (bf16[8,8,4,512]{3,2,1,0:T(4,128)(2,1)S(1)}, bf16[8,8,4,512]{3,2,1,0:T(4,128)(2,1)S(1)}, u32[]{:S(2)}, u32[]{:S(2)}) collective-permute-start(bf16[8,8,4,512]{3,2,1,0:T(4,128)(2,1)S(1)} %get-tuple-element.424), channel_id=1, source_target_pairs={{1,0},{2,1},{3,2},{4,3},{5,4},{6,5},{7,6},{8,7},{9,8},{10,9},{11,1... | collective-permute-start | bytes 786440 | tf_op jit(solution)/shard_map/while/body/eval_jaxpr/ppermute | solution.py:19
  183.9 3.3 collective-permute-start.1
  188.0 14.8 %collective-permute-start.2 = (bf16[8,8,8,512]{3,2,1,0:T(8,128)(2,1)S(1)}, bf16[8,8,8,512]{3,2,1,0:T(8,128)(2,1)S(1)}, u32[]{:S(2)}, u32[]{:S(2)}) collective-permute-start(bf16[8,8,8,512]{3,2,1,0:T(8,128)(2,1)S(1)} %get-tuple-element.522), channel_id=1, source_target_pairs={{0,32},{32,64},{64,96},{96,128},{128,160},{160,192},{192,224},{1,3... | collective-permute-start | bytes 1572872 | tf_op jit(solution)/shard_map/while/body/eval_jaxpr/ppermute | solution.py:29
  205.2 8.0 %collective-permute-start = (bf16[8,8,4,512]{3,2,1,0:T(4,128)(2,1)S(1)}, bf16[8,8,4,512]{3,2,1,0:T(4,128)(2,1)S(1)}, u32[]{:S(2)}, u32[]{:S(2)}) collective-permute-start(bf16[8,8,4,512]{3,2,1,0:T(4,128)(2,1)S(1)} %get-tuple-element.424), channel_id=1, source_target_pairs={{1,0},{2,1},{3,2},{4,3},{5,4},{6,5},{7,6},{8,7},{9,8},{10,9},{11,1... | collective-permute-start | bytes 786440 | tf_op jit(solution)/shard_map/while/body/eval_jaxpr/ppermute | solution.py:19
  212.0 3.3 collective-permute-start.1
  216.1 10.2 %collective-permute-start.2 = (bf16[8,8,8,512]{3,2,1,0:T(8,128)(2,1)S(1)}, bf16[8,8,8,512]{3,2,1,0:T(8,128)(2,1)S(1)}, u32[]{:S(2)}, u32[]{:S(2)}) collective-permute-start(bf16[8,8,8,512]{3,2,1,0:T(8,128)(2,1)S(1)} %get-tuple-element.522), channel_id=1, source_target_pairs={{0,32},{32,64},{64,96},{96,128},{128,160},{160,192},{192,224},{1,3... | collective-permute-start | bytes 1572872 | tf_op jit(solution)/shard_map/while/body/eval_jaxpr/ppermute | solution.py:29
  228.8 8.0 %collective-permute-start = (bf16[8,8,4,512]{3,2,1,0:T(4,128)(2,1)S(1)}, bf16[8,8,4,512]{3,2,1,0:T(4,128)(2,1)S(1)}, u32[]{:S(2)}, u32[]{:S(2)}) collective-permute-start(bf16[8,8,4,512]{3,2,1,0:T(4,128)(2,1)S(1)} %get-tuple-element.424), channel_id=1, source_target_pairs={{1,0},{2,1},{3,2},{4,3},{5,4},{6,5},{7,6},{8,7},{9,8},{10,9},{11,1... | collective-permute-start | bytes 786440 | tf_op jit(solution)/shard_map/while/body/eval_jaxpr/ppermute | solution.py:19
  235.6 3.3 collective-permute-start.1
  239.7 16.8 %collective-permute-start.2 = (bf16[8,8,8,512]{3,2,1,0:T(8,128)(2,1)S(1)}, bf16[8,8,8,512]{3,2,1,0:T(8,128)(2,1)S(1)}, u32[]{:S(2)}, u32[]{:S(2)}) collective-permute-start(bf16[8,8,8,512]{3,2,1,0:T(8,128)(2,1)S(1)} %get-tuple-element.522), channel_id=1, source_target_pairs={{0,32},{32,64},{64,96},{96,128},{128,160},{160,192},{192,224},{1,3... | collective-permute-start | bytes 1572872 | tf_op jit(solution)/shard_map/while/body/eval_jaxpr/ppermute | solution.py:29
  261.0 8.2 %collective-permute-start.3 = (bf16[8,8,4,512]{3,2,1,0:T(4,128)(2,1)}, bf16[8,8,4,512]{3,2,1,0:T(4,128)(2,1)}, u32[]{:S(2)}, u32[]{:S(2)}) collective-permute-start(bf16[8,8,4,512]{3,2,1,0:T(4,128)(2,1)} %get-tuple-element.439), channel_id=1, source_target_pairs={{1,0},{2,1},{3,2},{4,3},{5,4},{6,5},{7,6},{8,7},{9,8},{10,9},{11,1... | collective-permute-start | bytes 786440 | tf_op jit(solution)/shard_map/while/body/eval_jaxpr/ppermute | solution.py:19
  267.8 3.3 collective-permute-start.4
  272.8 11.8 %collective-permute-start.5 = (bf16[8,8,8,512]{3,2,1,0:T(8,128)(2,1)S(1)}, bf16[8,8,8,512]{3,2,1,0:T(8,128)(2,1)}, u32[]{:S(2)}, u32[]{:S(2)}) collective-permute-start(bf16[8,8,8,512]{3,2,1,0:T(8,128)(2,1)S(1)} %get-tuple-element.523), channel_id=1, source_target_pairs={{32,0},{64,32},{96,64},{128,96},{160,128},{192,160},{224,192},{33,... | collective-permute-start | bytes 1572872 | tf_op jit(solution)/shard_map/while/body/eval_jaxpr/ppermute | solution.py:29
  288.2 8.3 %collective-permute-start.3 = (bf16[8,8,4,512]{3,2,1,0:T(4,128)(2,1)}, bf16[8,8,4,512]{3,2,1,0:T(4,128)(2,1)}, u32[]{:S(2)}, u32[]{:S(2)}) collective-permute-start(bf16[8,8,4,512]{3,2,1,0:T(4,128)(2,1)} %get-tuple-element.439), channel_id=1, source_target_pairs={{1,0},{2,1},{3,2},{4,3},{5,4},{6,5},{7,6},{8,7},{9,8},{10,9},{11,1... | collective-permute-start | bytes 786440 | tf_op jit(solution)/shard_map/while/body/eval_jaxpr/ppermute | solution.py:19
  295.0 3.3 collective-permute-start.4
  300.1 13.6 %collective-permute-start.5 = (bf16[8,8,8,512]{3,2,1,0:T(8,128)(2,1)S(1)}, bf16[8,8,8,512]{3,2,1,0:T(8,128)(2,1)}, u32[]{:S(2)}, u32[]{:S(2)}) collective-permute-start(bf16[8,8,8,512]{3,2,1,0:T(8,128)(2,1)S(1)} %get-tuple-element.523), channel_id=1, source_target_pairs={{32,0},{64,32},{96,64},{128,96},{160,128},{192,160},{224,192},{33,... | collective-permute-start | bytes 1572872 | tf_op jit(solution)/shard_map/while/body/eval_jaxpr/ppermute | solution.py:29
  317.2 8.3 %collective-permute-start.3 = (bf16[8,8,4,512]{3,2,1,0:T(4,128)(2,1)}, bf16[8,8,4,512]{3,2,1,0:T(4,128)(2,1)}, u32[]{:S(2)}, u32[]{:S(2)}) collective-permute-start(bf16[8,8,4,512]{3,2,1,0:T(4,128)(2,1)} %get-tuple-element.439), channel_id=1, source_target_pairs={{1,0},{2,1},{3,2},{4,3},{5,4},{6,5},{7,6},{8,7},{9,8},{10,9},{11,1... | collective-permute-start | bytes 786440 | tf_op jit(solution)/shard_map/while/body/eval_jaxpr/ppermute | solution.py:19
  329.0 12.0 %collective-permute-start.5 = (bf16[8,8,8,512]{3,2,1,0:T(8,128)(2,1)S(1)}, bf16[8,8,8,512]{3,2,1,0:T(8,128)(2,1)}, u32[]{:S(2)}, u32[]{:S(2)}) collective-permute-start(bf16[8,8,8,512]{3,2,1,0:T(8,128)(2,1)S(1)} %get-tuple-element.523), channel_id=1, source_target_pairs={{32,0},{64,32},{96,64},{128,96},{160,128},{192,160},{224,192},{33,... | collective-permute-start | bytes 1572872 | tf_op jit(solution)/shard_map/while/body/eval_jaxpr/ppermute | solution.py:29
  344.6 8.3 %collective-permute-start.3 = (bf16[8,8,4,512]{3,2,1,0:T(4,128)(2,1)}, bf16[8,8,4,512]{3,2,1,0:T(4,128)(2,1)}, u32[]{:S(2)}, u32[]{:S(2)}) collective-permute-start(bf16[8,8,4,512]{3,2,1,0:T(4,128)(2,1)} %get-tuple-element.439), channel_id=1, source_target_pairs={{1,0},{2,1},{3,2},{4,3},{5,4},{6,5},{7,6},{8,7},{9,8},{10,9},{11,1... | collective-permute-start | bytes 786440 | tf_op jit(solution)/shard_map/while/body/eval_jaxpr/ppermute | solution.py:19
  356.4 13.6 %collective-permute-start.5 = (bf16[8,8,8,512]{3,2,1,0:T(8,128)(2,1)S(1)}, bf16[8,8,8,512]{3,2,1,0:T(8,128)(2,1)}, u32[]{:S(2)}, u32[]{:S(2)}) collective-permute-start(bf16[8,8,8,512]{3,2,1,0:T(8,128)(2,1)S(1)} %get-tuple-element.523), channel_id=1, source_target_pairs={{32,0},{64,32},{96,64},{128,96},{160,128},{192,160},{224,192},{33,... | collective-permute-start | bytes 1572872 | tf_op jit(solution)/shard_map/while/body/eval_jaxpr/ppermute | solution.py:29
  373.6 8.3 %collective-permute-start.3 = (bf16[8,8,4,512]{3,2,1,0:T(4,128)(2,1)}, bf16[8,8,4,512]{3,2,1,0:T(4,128)(2,1)}, u32[]{:S(2)}, u32[]{:S(2)}) collective-permute-start(bf16[8,8,4,512]{3,2,1,0:T(4,128)(2,1)} %get-tuple-element.439), channel_id=1, source_target_pairs={{1,0},{2,1},{3,2},{4,3},{5,4},{6,5},{7,6},{8,7},{9,8},{10,9},{11,1... | collective-permute-start | bytes 786440 | tf_op jit(solution)/shard_map/while/body/eval_jaxpr/ppermute | solution.py:19
  385.4 11.5 %collective-permute-start.5 = (bf16[8,8,8,512]{3,2,1,0:T(8,128)(2,1)S(1)}, bf16[8,8,8,512]{3,2,1,0:T(8,128)(2,1)}, u32[]{:S(2)}, u32[]{:S(2)}) collective-permute-start(bf16[8,8,8,512]{3,2,1,0:T(8,128)(2,1)S(1)} %get-tuple-element.523), channel_id=1, source_target_pairs={{32,0},{64,32},{96,64},{128,96},{160,128},{192,160},{224,192},{33,... | collective-permute-start | bytes 1572872 | tf_op jit(solution)/shard_map/while/body/eval_jaxpr/ppermute | solution.py:29
  400.5 8.3 %collective-permute-start.3 = (bf16[8,8,4,512]{3,2,1,0:T(4,128)(2,1)}, bf16[8,8,4,512]{3,2,1,0:T(4,128)(2,1)}, u32[]{:S(2)}, u32[]{:S(2)}) collective-permute-start(bf16[8,8,4,512]{3,2,1,0:T(4,128)(2,1)} %get-tuple-element.439), channel_id=1, source_target_pairs={{1,0},{2,1},{3,2},{4,3},{5,4},{6,5},{7,6},{8,7},{9,8},{10,9},{11,1... | collective-permute-start | bytes 786440 | tf_op jit(solution)/shard_map/while/body/eval_jaxpr/ppermute | solution.py:19
  412.4 14.0 %collective-permute-start.5 = (bf16[8,8,8,512]{3,2,1,0:T(8,128)(2,1)S(1)}, bf16[8,8,8,512]{3,2,1,0:T(8,128)(2,1)}, u32[]{:S(2)}, u32[]{:S(2)}) collective-permute-start(bf16[8,8,8,512]{3,2,1,0:T(8,128)(2,1)S(1)} %get-tuple-element.523), channel_id=1, source_target_pairs={{32,0},{64,32},{96,64},{128,96},{160,128},{192,160},{224,192},{33,... | collective-permute-start | bytes 1572872 | tf_op jit(solution)/shard_map/while/body/eval_jaxpr/ppermute | solution.py:29
  429.9 8.3 %collective-permute-start.3 = (bf16[8,8,4,512]{3,2,1,0:T(4,128)(2,1)}, bf16[8,8,4,512]{3,2,1,0:T(4,128)(2,1)}, u32[]{:S(2)}, u32[]{:S(2)}) collective-permute-start(bf16[8,8,4,512]{3,2,1,0:T(4,128)(2,1)} %get-tuple-element.439), channel_id=1, source_target_pairs={{1,0},{2,1},{3,2},{4,3},{5,4},{6,5},{7,6},{8,7},{9,8},{10,9},{11,1... | collective-permute-start | bytes 786440 | tf_op jit(solution)/shard_map/while/body/eval_jaxpr/ppermute | solution.py:19
  441.8 56.5 %collective-permute-start.5 = (bf16[8,8,8,512]{3,2,1,0:T(8,128)(2,1)S(1)}, bf16[8,8,8,512]{3,2,1,0:T(8,128)(2,1)}, u32[]{:S(2)}, u32[]{:S(2)}) collective-permute-start(bf16[8,8,8,512]{3,2,1,0:T(8,128)(2,1)S(1)} %get-tuple-element.523), channel_id=1, source_target_pairs={{32,0},{64,32},{96,64},{128,96},{160,128},{192,160},{224,192},{33,... | collective-permute-start | bytes 1572872 | tf_op jit(solution)/shard_map/while/body/eval_jaxpr/ppermute | solution.py:29
  501.8 8.3 %collective-permute-start.3 = (bf16[8,8,4,512]{3,2,1,0:T(4,128)(2,1)}, bf16[8,8,4,512]{3,2,1,0:T(4,128)(2,1)}, u32[]{:S(2)}, u32[]{:S(2)}) collective-permute-start(bf16[8,8,4,512]{3,2,1,0:T(4,128)(2,1)} %get-tuple-element.439), channel_id=1, source_target_pairs={{1,0},{2,1},{3,2},{4,3},{5,4},{6,5},{7,6},{8,7},{9,8},{10,9},{11,1... | collective-permute-start | bytes 786440 | tf_op jit(solution)/shard_map/while/body/eval_jaxpr/ppermute | solution.py:19
  520.4 11.5 %collective-permute-start.5 = (bf16[8,8,8,512]{3,2,1,0:T(8,128)(2,1)S(1)}, bf16[8,8,8,512]{3,2,1,0:T(8,128)(2,1)}, u32[]{:S(2)}, u32[]{:S(2)}) collective-permute-start(bf16[8,8,8,512]{3,2,1,0:T(8,128)(2,1)S(1)} %get-tuple-element.523), channel_id=1, source_target_pairs={{32,0},{64,32},{96,64},{128,96},{160,128},{192,160},{224,192},{33,... | collective-permute-start | bytes 1572872 | tf_op jit(solution)/shard_map/while/body/eval_jaxpr/ppermute | solution.py:29
  535.5 8.3 %collective-permute-start.3 = (bf16[8,8,4,512]{3,2,1,0:T(4,128)(2,1)}, bf16[8,8,4,512]{3,2,1,0:T(4,128)(2,1)}, u32[]{:S(2)}, u32[]{:S(2)}) collective-permute-start(bf16[8,8,4,512]{3,2,1,0:T(4,128)(2,1)} %get-tuple-element.439), channel_id=1, source_target_pairs={{1,0},{2,1},{3,2},{4,3},{5,4},{6,5},{7,6},{8,7},{9,8},{10,9},{11,1... | collective-permute-start | bytes 786440 | tf_op jit(solution)/shard_map/while/body/eval_jaxpr/ppermute | solution.py:19
  554.2 10.0 %collective-permute-start.5 = (bf16[8,8,8,512]{3,2,1,0:T(8,128)(2,1)S(1)}, bf16[8,8,8,512]{3,2,1,0:T(8,128)(2,1)}, u32[]{:S(2)}, u32[]{:S(2)}) collective-permute-start(bf16[8,8,8,512]{3,2,1,0:T(8,128)(2,1)S(1)} %get-tuple-element.523), channel_id=1, source_target_pairs={{32,0},{64,32},{96,64},{128,96},{160,128},{192,160},{224,192},{33,... | collective-permute-start | bytes 1572872 | tf_op jit(solution)/shard_map/while/body/eval_jaxpr/ppermute | solution.py:29
  (15 other events, 986.3 us)
Sparse Core Ops, SparseCore 0:
  565.5 68.8 all-reduce.3
where the time goes:
time: 799 us; the launch traced here: 797 us
  waiting for transfers between devices  322 us (40%)
  starting transfers between devices  193 us (24%)
  blocking collectives  153 us (19%)
  other arithmetic  49.3 us (6%)
  local copies, waits for them, and re-layouts  35.4 us (4%)
  matrix products  17.6 us (2%)
  between operations  14.2 us (2%)
  loops' own time  12.5 us (2%)
    ppermute x18, waiting for transfers between devices, from_behind(): return lax.ppermute(shard, axis, pairs)  193 us
    ppermute x18, starting transfers between devices, padded(): lax.ppermute(head, axis, [((i + 1) % count, i) for i in range(count)])  125 us
    psum x1, blocking collectives, body(): projection = lax.psum(part_projection, ('section', 'lon'))  79.2 us
    psum x1, blocking collectives, body(): residual_gram = lax.psum(part_gram, ('section', 'lon'))  73.3 us
    psum x1, waiting for transfers between devices, broadcast(): return lax.psum(jnp.where(mine, shard, jnp.zeros_like(shard)), axis)  67.9 us
    ppermute x18, starting transfers between devices, from_behind(): return lax.ppermute(shard, axis, pairs)  67.9 us
    ppermute x18, waiting for transfers between devices, padded(): lax.ppermute(tail, axis, [(i, (i + 1) % count) for i in range(count)])  33.5 us
    ppermute x18, waiting for transfers between devices, padded(): lax.ppermute(head, axis, [((i + 1) % count, i) for i in range(count)])  27.4 us
  transfers between devices with their start and end apart: 55, of which 55 were waited for; matrix products, arithmetic and copies ran while one was open for 1% of the time, Pallas kernels for 0%

commit v1 on v0

--- a/solution.py
+++ b/solution.py
@@ -159,7 +159,8 @@
     projection = lax.psum(part_projection, ("section", "lon"))
     residual_rows = shifted - jnp.dot(projection.T, block_flat, precision=high)
     part_gram = jnp.dot(residual_rows, residual_rows.T, precision=high) / cell_count
-    residual_gram = lax.psum(part_gram, ("section", "lon"))
+    block_now = lax.psum(part_gram, "section")
+    residual_gram = lax.psum(block_now, "lon")
     return (residual_rows.reshape(own_block.shape), projection, residual_gram)
 
 

time: 799 us -> 807 us (1.010)
    psum x1 -> x2, blocking collectives: 73.3 us -> 79.6 us  [the longest x1 68 us: body(): residual_gram = lax.psum(block_now, 'lon')]
where the time goes in v1:
time: 807 us; the launch traced here: 805 us
  waiting for transfers between devices  322 us (40%)
  starting transfers between devices  193 us (24%)
  blocking collectives  159 us (20%)
  other arithmetic  49.3 us (6%)
  local copies, waits for them, and re-layouts  36 us (4%)
  matrix products  17.6 us (2%)
  between operations  14.2 us (2%)
  loops' own time  13.3 us (2%)
    ppermute x18, waiting for transfers between devices, from_behind(): return lax.ppermute(shard, axis, pairs)  193 us
    ppermute x18, starting transfers between devices, padded(): lax.ppermute(head, axis, [((i + 1) % count, i) for i in range(count)])  125 us
    psum x1, blocking collectives, body(): projection = lax.psum(part_projection, ('section', 'lon'))  79.2 us
    psum x1, blocking collectives, body(): residual_gram = lax.psum(block_now, 'lon')  68 us
    ppermute x18, starting transfers between devices, from_behind(): return lax.ppermute(shard, axis, pairs)  67.9 us
    psum x1, waiting for transfers between devices, broadcast(): return lax.psum(jnp.where(mine, shard, jnp.zeros_like(shard)), axis)  67.9 us
    ppermute x18, waiting for transfers between devices, padded(): lax.ppermute(tail, axis, [(i, (i + 1) % count) for i in range(count)])  33.5 us
    ppermute x18, waiting for transfers between devices, padded(): lax.ppermute(head, axis, [((i + 1) % count, i) for i in range(count)])  27.4 us
  transfers between devices with their start and end apart: 55, of which 55 were waited for; matrix products, arithmetic and copies ran while one was open for 1% of the time, Pallas kernels for 0%

profile of v1, /device:TPU:1, one launch (start us, length us, event | category | flops | bytes accessed | tf_op | source)
XLA Modules:
  0.0 804.6 jit_solution(9021814714355442907)
XLA Ops:
  8.3 249.6 %while.27 = (s32[]{:T(128)}, bf16[8,8,8,512]{3,2,1,0:T(8,128)(2,1)S(1)}, bf16[2,8,8,8,512]{4,3,2,1,0:T(8,128)(2,1)S(1)}, s32[9]{0:T(128)S(1)}, s32[]{:T(128)}, /...) while((s32[]{:T(128)}, ...), condition=%wide.region_3.4_spmd, body=%wide.region_0.3_spmd.sunk | while | flops 2422734848 | bytes 67240344 | solution.py:106
  18.8 6.5 conditional.4
  26.9 5.8 collective-permute-done.2
  35.4 8.7 %collective-permute-start = (bf16[8,8,4,512]{3,2,1,0:T(4,128)(2,1)S(1)}, bf16[8,8,4,512]{3,2,1,0:T(4,128)(2,1)S(1)}, u32[]{:S(2)}, u32[]{:S(2)}) collective-permute-start(bf16[8,8,4,512]{3,2,1,0:T(4,128)(2,1)S(1)} %get-tuple-element.424), channel_id=1, source_target_pairs={{1,0},{2,1},{3,2},{4,3},{5,4},{6,5},{7,6},{8,7},{9,8},{10,9},{11,1... | collective-permute-start | bytes 786440 | tf_op jit(solution)/shard_map/while/body/eval_jaxpr/ppermute | solution.py:19
  48.7 6.5 conditional.4
  59.3 5.8 collective-permute-done.2
  67.8 9.0 %collective-permute-start = (bf16[8,8,4,512]{3,2,1,0:T(4,128)(2,1)S(1)}, bf16[8,8,4,512]{3,2,1,0:T(4,128)(2,1)S(1)}, u32[]{:S(2)}, u32[]{:S(2)}) collective-permute-start(bf16[8,8,4,512]{3,2,1,0:T(4,128)(2,1)S(1)} %get-tuple-element.424), channel_id=1, source_target_pairs={{1,0},{2,1},{3,2},{4,3},{5,4},{6,5},{7,6},{8,7},{9,8},{10,9},{11,1... | collective-permute-start | bytes 786440 | tf_op jit(solution)/shard_map/while/body/eval_jaxpr/ppermute | solution.py:19
  80.9 10.6 %collective-permute-start.2 = (bf16[8,8,8,512]{3,2,1,0:T(8,128)(2,1)S(1)}, bf16[8,8,8,512]{3,2,1,0:T(8,128)(2,1)S(1)}, u32[]{:S(2)}, u32[]{:S(2)}) collective-permute-start(bf16[8,8,8,512]{3,2,1,0:T(8,128)(2,1)S(1)} %get-tuple-element.522), channel_id=1, source_target_pairs={{0,32},{32,64},{64,96},{96,128},{128,160},{160,192},{192,224},{1,3... | collective-permute-start | bytes 1572872 | tf_op jit(solution)/shard_map/while/body/eval_jaxpr/ppermute | solution.py:29
  91.7 5.8 collective-permute-done.2
  100.2 8.1 %collective-permute-start = (bf16[8,8,4,512]{3,2,1,0:T(4,128)(2,1)S(1)}, bf16[8,8,4,512]{3,2,1,0:T(4,128)(2,1)S(1)}, u32[]{:S(2)}, u32[]{:S(2)}) collective-permute-start(bf16[8,8,4,512]{3,2,1,0:T(4,128)(2,1)S(1)} %get-tuple-element.424), channel_id=1, source_target_pairs={{1,0},{2,1},{3,2},{4,3},{5,4},{6,5},{7,6},{8,7},{9,8},{10,9},{11,1... | collective-permute-start | bytes 786440 | tf_op jit(solution)/shard_map/while/body/eval_jaxpr/ppermute | solution.py:19
  116.7 5.8 collective-permute-done.2
  125.2 7.2 collective-permute-start
  136.4 8.7 %collective-permute-start.2 = (bf16[8,8,8,512]{3,2,1,0:T(8,128)(2,1)S(1)}, bf16[8,8,8,512]{3,2,1,0:T(8,128)(2,1)S(1)}, u32[]{:S(2)}, u32[]{:S(2)}) collective-permute-start(bf16[8,8,8,512]{3,2,1,0:T(8,128)(2,1)S(1)} %get-tuple-element.522), channel_id=1, source_target_pairs={{0,32},{32,64},{64,96},{96,128},{128,160},{160,192},{192,224},{1,3... | collective-permute-start | bytes 1572872 | tf_op jit(solution)/shard_map/while/body/eval_jaxpr/ppermute | solution.py:29
  145.3 5.8 collective-permute-done.2
  153.8 7.4 collective-permute-start
  169.7 5.8 collective-permute-done.2
  178.1 6.8 collective-permute-start
  189.0 8.7 %collective-permute-start.2 = (bf16[8,8,8,512]{3,2,1,0:T(8,128)(2,1)S(1)}, bf16[8,8,8,512]{3,2,1,0:T(8,128)(2,1)S(1)}, u32[]{:S(2)}, u32[]{:S(2)}) collective-permute-start(bf16[8,8,8,512]{3,2,1,0:T(8,128)(2,1)S(1)} %get-tuple-element.522), channel_id=1, source_target_pairs={{0,32},{32,64},{64,96},{96,128},{128,160},{160,192},{192,224},{1,3... | collective-permute-start | bytes 1572872 | tf_op jit(solution)/shard_map/while/body/eval_jaxpr/ppermute | solution.py:29
  197.9 5.8 collective-permute-done.2
  206.4 6.8 collective-permute-start
  221.7 5.8 collective-permute-done.2
  230.1 6.8 collective-permute-start
  241.0 10.7 %collective-permute-start.2 = (bf16[8,8,8,512]{3,2,1,0:T(8,128)(2,1)S(1)}, bf16[8,8,8,512]{3,2,1,0:T(8,128)(2,1)S(1)}, u32[]{:S(2)}, u32[]{:S(2)}) collective-permute-start(bf16[8,8,8,512]{3,2,1,0:T(8,128)(2,1)S(1)} %get-tuple-element.522), channel_id=1, source_target_pairs={{0,32},{32,64},{64,96},{96,128},{128,160},{160,192},{192,224},{1,3... | collective-permute-start | bytes 1572872 | tf_op jit(solution)/shard_map/while/body/eval_jaxpr/ppermute | solution.py:29
  258.8 306.7 %while.28 = (s32[]{:T(128)}, bf16[8,8,8,512]{3,2,1,0:T(8,128)(2,1)}, bf16[2,8,8,8,512]{4,3,2,1,0:T(8,128)(2,1)S(1)}, s32[9]{0:T(128)S(1)}, s32[]{:T(128)}, /*ind...) while((s32[]{:T(128)}, ...), condition=%wide.region_7.8_spmd, body=%wide.region_4.7_spmd.sunk | while | flops 2424045568 | bytes 67764888 | solution.py:138
  262.3 6.7 collective-permute-start.3
  275.7 10.3 %collective-permute-done.5 = bf16[8,8,8,512]{3,2,1,0:T(8,128)(2,1)} collective-permute-done((bf16[8,8,8,512]{3,2,1,0:T(8,128)(2,1)S(1)}, bf16[8,8,8,512]{3,2,1,0:T(8,128)(2,1)}, u32[]{:S(2)}, u32[]{:S(2)}) %collective-permute-start.5) | collective-permute-done | bytes 524320 | tf_op jit(solution)/shard_map/while/body/eval_jaxpr/ppermute | solution.py:29
  289.5 6.8 collective-permute-start.3
  302.9 12.0 %collective-permute-done.5 = bf16[8,8,8,512]{3,2,1,0:T(8,128)(2,1)} collective-permute-done((bf16[8,8,8,512]{3,2,1,0:T(8,128)(2,1)S(1)}, bf16[8,8,8,512]{3,2,1,0:T(8,128)(2,1)}, u32[]{:S(2)}, u32[]{:S(2)}) %collective-permute-start.5) | collective-permute-done | bytes 524320 | tf_op jit(solution)/shard_map/while/body/eval_jaxpr/ppermute | solution.py:29
  318.5 6.8 collective-permute-start.3
  331.9 10.5 %collective-permute-done.5 = bf16[8,8,8,512]{3,2,1,0:T(8,128)(2,1)} collective-permute-done((bf16[8,8,8,512]{3,2,1,0:T(8,128)(2,1)S(1)}, bf16[8,8,8,512]{3,2,1,0:T(8,128)(2,1)}, u32[]{:S(2)}, u32[]{:S(2)}) %collective-permute-start.5) | collective-permute-done | bytes 524320 | tf_op jit(solution)/shard_map/while/body/eval_jaxpr/ppermute | solution.py:29
  345.9 6.8 collective-permute-start.3
  359.3 12.0 %collective-permute-done.5 = bf16[8,8,8,512]{3,2,1,0:T(8,128)(2,1)} collective-permute-done((bf16[8,8,8,512]{3,2,1,0:T(8,128)(2,1)S(1)}, bf16[8,8,8,512]{3,2,1,0:T(8,128)(2,1)}, u32[]{:S(2)}, u32[]{:S(2)}) %collective-permute-start.5) | collective-permute-done | bytes 524320 | tf_op jit(solution)/shard_map/while/body/eval_jaxpr/ppermute | solution.py:29
  374.9 6.8 collective-permute-start.3
  388.3 10.0 %collective-permute-done.5 = bf16[8,8,8,512]{3,2,1,0:T(8,128)(2,1)} collective-permute-done((bf16[8,8,8,512]{3,2,1,0:T(8,128)(2,1)S(1)}, bf16[8,8,8,512]{3,2,1,0:T(8,128)(2,1)}, u32[]{:S(2)}, u32[]{:S(2)}) %collective-permute-start.5) | collective-permute-done | bytes 524320 | tf_op jit(solution)/shard_map/while/body/eval_jaxpr/ppermute | solution.py:29
  401.8 6.8 collective-permute-start.3
  415.2 12.5 %collective-permute-done.5 = bf16[8,8,8,512]{3,2,1,0:T(8,128)(2,1)} collective-permute-done((bf16[8,8,8,512]{3,2,1,0:T(8,128)(2,1)S(1)}, bf16[8,8,8,512]{3,2,1,0:T(8,128)(2,1)}, u32[]{:S(2)}, u32[]{:S(2)}) %collective-permute-start.5) | collective-permute-done | bytes 524320 | tf_op jit(solution)/shard_map/while/body/eval_jaxpr/ppermute | solution.py:29
  431.3 6.8 collective-permute-start.3
  444.6 54.9 %collective-permute-done.5 = bf16[8,8,8,512]{3,2,1,0:T(8,128)(2,1)} collective-permute-done((bf16[8,8,8,512]{3,2,1,0:T(8,128)(2,1)S(1)}, bf16[8,8,8,512]{3,2,1,0:T(8,128)(2,1)}, u32[]{:S(2)}, u32[]{:S(2)}) %collective-permute-start.5) | collective-permute-done | bytes 524320 | tf_op jit(solution)/shard_map/while/body/eval_jaxpr/ppermute | solution.py:29
  503.1 6.8 collective-permute-start.3
  514.9 6.8 conditional.5
  523.3 10.0 %collective-permute-done.5 = bf16[8,8,8,512]{3,2,1,0:T(8,128)(2,1)} collective-permute-done((bf16[8,8,8,512]{3,2,1,0:T(8,128)(2,1)S(1)}, bf16[8,8,8,512]{3,2,1,0:T(8,128)(2,1)}, u32[]{:S(2)}, u32[]{:S(2)}) %collective-permute-start.5) | collective-permute-done | bytes 524320 | tf_op jit(solution)/shard_map/while/body/eval_jaxpr/ppermute | solution.py:29
  536.8 6.8 collective-permute-start.3
  548.6 6.8 conditional.5
  557.0 8.5 %collective-permute-done.5 = bf16[8,8,8,512]{3,2,1,0:T(8,128)(2,1)} collective-permute-done((bf16[8,8,8,512]{3,2,1,0:T(8,128)(2,1)S(1)}, bf16[8,8,8,512]{3,2,1,0:T(8,128)(2,1)}, u32[]{:S(2)}, u32[]{:S(2)}) %collective-permute-start.5) | collective-permute-done | bytes 524320 | tf_op jit(solution)/shard_map/while/body/eval_jaxpr/ppermute | solution.py:29
  567.7 67.9 %all-reduce.4.cloned.1.call-done = bf16[16,8,8,512]{3,2,0,1:T(8,128)(2,1)} async-done(((bf16[16,8,8,512]{3,2,0,1:T(8,128)(2,1)}), bf16[16,8,8,512]{3,2,0,1:T(8,128)(2,1)}) %all-reduce.4.cloned.1.call-update) | async-done | bytes 1048592 | tf_op jit(solution)/shard_map/psum | solution.py:34
  637.3 79.2 %psum.29 = f32[16,16]{1,0:T(8,128)S(1)} all-reduce(f32[16,16]{1,0:T(8,128)S(1)} %convolution_multiply_fusion.1), channel_id=1, replica_groups=mesh['section'=8,'lon'=32] {'section','lon'}, use_global_device_ids=true, to_apply=%region_9.10 | all-reduce | flops 256 | bytes 2048 | tf_op jit(solution)/shard_map/psum | solution.py:159
  718.1 11.6 %psum.30 = f32[16,16]{1,0:T(8,128)S(1)} all-reduce(f32[16,16]{1,0:T(8,128)S(1)} %convolution_multiply_fusion), channel_id=1, replica_groups=mesh['section'=8,'lon'=32] {'section'}, use_global_device_ids=true, to_apply=%region_10.11 | all-reduce | flops 256 | bytes 2048 | tf_op jit(solution)/shard_map/psum | solution.py:162
  729.7 68.0 %psum.31 = f32[16,16]{1,0:T(8,128)} all-reduce(f32[16,16]{1,0:T(8,128)S(1)} %psum.30), channel_id=1, replica_groups=mesh['section'=8,'lon'=32] {'lon'}, use_global_device_ids=true, to_apply=%region_11.12 | all-reduce | flops 256 | bytes 2048 | tf_op jit(solution)/shard_map/psum | solution.py:163
  (287 shorter events, 203.1 us)
Async XLA Ops:
  7.2 628.4 %all-reduce.4.cloned.1.call-start = ((), (), s32[]{:S(2)}) async-start(), calls=%async_computation | async-start | bytes 2097152 | tf_op jit(solution)/shard_map/psum | solution.py:34
  10.9 6.7 collective-permute-start
  14.2 4.0 collective-permute-start.1
  25.4 7.4 collective-permute-start.2
  35.4 11.0 %collective-permute-start = (bf16[8,8,4,512]{3,2,1,0:T(4,128)(2,1)S(1)}, bf16[8,8,4,512]{3,2,1,0:T(4,128)(2,1)S(1)}, u32[]{:S(2)}, u32[]{:S(2)}) collective-permute-start(bf16[8,8,4,512]{3,2,1,0:T(4,128)(2,1)S(1)} %get-tuple-element.424), channel_id=1, source_target_pairs={{1,0},{2,1},{3,2},{4,3},{5,4},{6,5},{7,6},{8,7},{9,8},{10,9},{11,1... | collective-permute-start | bytes 786440 | tf_op jit(solution)/shard_map/while/body/eval_jaxpr/ppermute | solution.py:19
  44.1 3.9 collective-permute-start.1
  55.2 9.9 %collective-permute-start.2 = (bf16[8,8,8,512]{3,2,1,0:T(8,128)(2,1)S(1)}, bf16[8,8,8,512]{3,2,1,0:T(8,128)(2,1)S(1)}, u32[]{:S(2)}, u32[]{:S(2)}) collective-permute-start(bf16[8,8,8,512]{3,2,1,0:T(8,128)(2,1)S(1)} %get-tuple-element.522), channel_id=1, source_target_pairs={{0,32},{32,64},{64,96},{96,128},{128,160},{160,192},{192,224},{1,3... | collective-permute-start | bytes 1572872 | tf_op jit(solution)/shard_map/while/body/eval_jaxpr/ppermute | solution.py:29
  67.8 10.2 %collective-permute-start = (bf16[8,8,4,512]{3,2,1,0:T(4,128)(2,1)S(1)}, bf16[8,8,4,512]{3,2,1,0:T(4,128)(2,1)S(1)}, u32[]{:S(2)}, u32[]{:S(2)}) collective-permute-start(bf16[8,8,4,512]{3,2,1,0:T(4,128)(2,1)S(1)} %get-tuple-element.424), channel_id=1, source_target_pairs={{1,0},{2,1},{3,2},{4,3},{5,4},{6,5},{7,6},{8,7},{9,8},{10,9},{11,1... | collective-permute-start | bytes 786440 | tf_op jit(solution)/shard_map/while/body/eval_jaxpr/ppermute | solution.py:19
  76.8 3.3 collective-permute-start.1
  80.9 16.7 %collective-permute-start.2 = (bf16[8,8,8,512]{3,2,1,0:T(8,128)(2,1)S(1)}, bf16[8,8,8,512]{3,2,1,0:T(8,128)(2,1)S(1)}, u32[]{:S(2)}, u32[]{:S(2)}) collective-permute-start(bf16[8,8,8,512]{3,2,1,0:T(8,128)(2,1)S(1)} %get-tuple-element.522), channel_id=1, source_target_pairs={{0,32},{32,64},{64,96},{96,128},{128,160},{160,192},{192,224},{1,3... | collective-permute-start | bytes 1572872 | tf_op jit(solution)/shard_map/while/body/eval_jaxpr/ppermute | solution.py:29
  100.2 9.3 %collective-permute-start = (bf16[8,8,4,512]{3,2,1,0:T(4,128)(2,1)S(1)}, bf16[8,8,4,512]{3,2,1,0:T(4,128)(2,1)S(1)}, u32[]{:S(2)}, u32[]{:S(2)}) collective-permute-start(bf16[8,8,4,512]{3,2,1,0:T(4,128)(2,1)S(1)} %get-tuple-element.424), channel_id=1, source_target_pairs={{1,0},{2,1},{3,2},{4,3},{5,4},{6,5},{7,6},{8,7},{9,8},{10,9},{11,1... | collective-permute-start | bytes 786440 | tf_op jit(solution)/shard_map/while/body/eval_jaxpr/ppermute | solution.py:19
  108.3 3.3 collective-permute-start.1
  112.3 10.2 %collective-permute-start.2 = (bf16[8,8,8,512]{3,2,1,0:T(8,128)(2,1)S(1)}, bf16[8,8,8,512]{3,2,1,0:T(8,128)(2,1)S(1)}, u32[]{:S(2)}, u32[]{:S(2)}) collective-permute-start(bf16[8,8,8,512]{3,2,1,0:T(8,128)(2,1)S(1)} %get-tuple-element.522), channel_id=1, source_target_pairs={{0,32},{32,64},{64,96},{96,128},{128,160},{160,192},{192,224},{1,3... | collective-permute-start | bytes 1572872 | tf_op jit(solution)/shard_map/while/body/eval_jaxpr/ppermute | solution.py:29
  125.2 8.3 %collective-permute-start = (bf16[8,8,4,512]{3,2,1,0:T(4,128)(2,1)S(1)}, bf16[8,8,4,512]{3,2,1,0:T(4,128)(2,1)S(1)}, u32[]{:S(2)}, u32[]{:S(2)}) collective-permute-start(bf16[8,8,4,512]{3,2,1,0:T(4,128)(2,1)S(1)} %get-tuple-element.424), channel_id=1, source_target_pairs={{1,0},{2,1},{3,2},{4,3},{5,4},{6,5},{7,6},{8,7},{9,8},{10,9},{11,1... | collective-permute-start | bytes 786440 | tf_op jit(solution)/shard_map/while/body/eval_jaxpr/ppermute | solution.py:19
  132.3 3.3 collective-permute-start.1
  136.4 14.8 %collective-permute-start.2 = (bf16[8,8,8,512]{3,2,1,0:T(8,128)(2,1)S(1)}, bf16[8,8,8,512]{3,2,1,0:T(8,128)(2,1)S(1)}, u32[]{:S(2)}, u32[]{:S(2)}) collective-permute-start(bf16[8,8,8,512]{3,2,1,0:T(8,128)(2,1)S(1)} %get-tuple-element.522), channel_id=1, source_target_pairs={{0,32},{32,64},{64,96},{96,128},{128,160},{160,192},{192,224},{1,3... | collective-permute-start | bytes 1572872 | tf_op jit(solution)/shard_map/while/body/eval_jaxpr/ppermute | solution.py:29
  153.8 8.6 %collective-permute-start = (bf16[8,8,4,512]{3,2,1,0:T(4,128)(2,1)S(1)}, bf16[8,8,4,512]{3,2,1,0:T(4,128)(2,1)S(1)}, u32[]{:S(2)}, u32[]{:S(2)}) collective-permute-start(bf16[8,8,4,512]{3,2,1,0:T(4,128)(2,1)S(1)} %get-tuple-element.424), channel_id=1, source_target_pairs={{1,0},{2,1},{3,2},{4,3},{5,4},{6,5},{7,6},{8,7},{9,8},{10,9},{11,1... | collective-permute-start | bytes 786440 | tf_op jit(solution)/shard_map/while/body/eval_jaxpr/ppermute | solution.py:19
  161.2 3.3 collective-permute-start.1
  165.3 10.2 %collective-permute-start.2 = (bf16[8,8,8,512]{3,2,1,0:T(8,128)(2,1)S(1)}, bf16[8,8,8,512]{3,2,1,0:T(8,128)(2,1)S(1)}, u32[]{:S(2)}, u32[]{:S(2)}) collective-permute-start(bf16[8,8,8,512]{3,2,1,0:T(8,128)(2,1)S(1)} %get-tuple-element.522), channel_id=1, source_target_pairs={{0,32},{32,64},{64,96},{96,128},{128,160},{160,192},{192,224},{1,3... | collective-permute-start | bytes 1572872 | tf_op jit(solution)/shard_map/while/body/eval_jaxpr/ppermute | solution.py:29
  178.1 8.0 collective-permute-start
  184.9 3.3 collective-permute-start.1
  189.0 14.8 %collective-permute-start.2 = (bf16[8,8,8,512]{3,2,1,0:T(8,128)(2,1)S(1)}, bf16[8,8,8,512]{3,2,1,0:T(8,128)(2,1)S(1)}, u32[]{:S(2)}, u32[]{:S(2)}) collective-permute-start(bf16[8,8,8,512]{3,2,1,0:T(8,128)(2,1)S(1)} %get-tuple-element.522), channel_id=1, source_target_pairs={{0,32},{32,64},{64,96},{96,128},{128,160},{160,192},{192,224},{1,3... | collective-permute-start | bytes 1572872 | tf_op jit(solution)/shard_map/while/body/eval_jaxpr/ppermute | solution.py:29
  206.4 8.0 collective-permute-start
  213.2 3.3 collective-permute-start.1
  217.3 10.2 %collective-permute-start.2 = (bf16[8,8,8,512]{3,2,1,0:T(8,128)(2,1)S(1)}, bf16[8,8,8,512]{3,2,1,0:T(8,128)(2,1)S(1)}, u32[]{:S(2)}, u32[]{:S(2)}) collective-permute-start(bf16[8,8,8,512]{3,2,1,0:T(8,128)(2,1)S(1)} %get-tuple-element.522), channel_id=1, source_target_pairs={{0,32},{32,64},{64,96},{96,128},{128,160},{160,192},{192,224},{1,3... | collective-permute-start | bytes 1572872 | tf_op jit(solution)/shard_map/while/body/eval_jaxpr/ppermute | solution.py:29
  230.1 8.0 collective-permute-start
  236.9 3.3 collective-permute-start.1
  241.0 16.8 %collective-permute-start.2 = (bf16[8,8,8,512]{3,2,1,0:T(8,128)(2,1)S(1)}, bf16[8,8,8,512]{3,2,1,0:T(8,128)(2,1)S(1)}, u32[]{:S(2)}, u32[]{:S(2)}) collective-permute-start(bf16[8,8,8,512]{3,2,1,0:T(8,128)(2,1)S(1)} %get-tuple-element.522), channel_id=1, source_target_pairs={{0,32},{32,64},{64,96},{96,128},{128,160},{160,192},{192,224},{1,3... | collective-permute-start | bytes 1572872 | tf_op jit(solution)/shard_map/while/body/eval_jaxpr/ppermute | solution.py:29
  262.3 8.2 %collective-permute-start.3 = (bf16[8,8,4,512]{3,2,1,0:T(4,128)(2,1)}, bf16[8,8,4,512]{3,2,1,0:T(4,128)(2,1)}, u32[]{:S(2)}, u32[]{:S(2)}) collective-permute-start(bf16[8,8,4,512]{3,2,1,0:T(4,128)(2,1)} %get-tuple-element.439), channel_id=1, source_target_pairs={{1,0},{2,1},{3,2},{4,3},{5,4},{6,5},{7,6},{8,7},{9,8},{10,9},{11,1... | collective-permute-start | bytes 786440 | tf_op jit(solution)/shard_map/while/body/eval_jaxpr/ppermute | solution.py:19
  269.1 3.3 collective-permute-start.4
  274.2 11.8 %collective-permute-start.5 = (bf16[8,8,8,512]{3,2,1,0:T(8,128)(2,1)S(1)}, bf16[8,8,8,512]{3,2,1,0:T(8,128)(2,1)}, u32[]{:S(2)}, u32[]{:S(2)}) collective-permute-start(bf16[8,8,8,512]{3,2,1,0:T(8,128)(2,1)S(1)} %get-tuple-element.523), channel_id=1, source_target_pairs={{32,0},{64,32},{96,64},{128,96},{160,128},{192,160},{224,192},{33,... | collective-permute-start | bytes 1572872 | tf_op jit(solution)/shard_map/while/body/eval_jaxpr/ppermute | solution.py:29
  289.5 8.3 %collective-permute-start.3 = (bf16[8,8,4,512]{3,2,1,0:T(4,128)(2,1)}, bf16[8,8,4,512]{3,2,1,0:T(4,128)(2,1)}, u32[]{:S(2)}, u32[]{:S(2)}) collective-permute-start(bf16[8,8,4,512]{3,2,1,0:T(4,128)(2,1)} %get-tuple-element.439), channel_id=1, source_target_pairs={{1,0},{2,1},{3,2},{4,3},{5,4},{6,5},{7,6},{8,7},{9,8},{10,9},{11,1... | collective-permute-start | bytes 786440 | tf_op jit(solution)/shard_map/while/body/eval_jaxpr/ppermute | solution.py:19
  296.3 3.3 collective-permute-start.4
  301.4 13.6 %collective-permute-start.5 = (bf16[8,8,8,512]{3,2,1,0:T(8,128)(2,1)S(1)}, bf16[8,8,8,512]{3,2,1,0:T(8,128)(2,1)}, u32[]{:S(2)}, u32[]{:S(2)}) collective-permute-start(bf16[8,8,8,512]{3,2,1,0:T(8,128)(2,1)S(1)} %get-tuple-element.523), channel_id=1, source_target_pairs={{32,0},{64,32},{96,64},{128,96},{160,128},{192,160},{224,192},{33,... | collective-permute-start | bytes 1572872 | tf_op jit(solution)/shard_map/while/body/eval_jaxpr/ppermute | solution.py:29
  318.5 8.3 %collective-permute-start.3 = (bf16[8,8,4,512]{3,2,1,0:T(4,128)(2,1)}, bf16[8,8,4,512]{3,2,1,0:T(4,128)(2,1)}, u32[]{:S(2)}, u32[]{:S(2)}) collective-permute-start(bf16[8,8,4,512]{3,2,1,0:T(4,128)(2,1)} %get-tuple-element.439), channel_id=1, source_target_pairs={{1,0},{2,1},{3,2},{4,3},{5,4},{6,5},{7,6},{8,7},{9,8},{10,9},{11,1... | collective-permute-start | bytes 786440 | tf_op jit(solution)/shard_map/while/body/eval_jaxpr/ppermute | solution.py:19
  330.3 12.0 %collective-permute-start.5 = (bf16[8,8,8,512]{3,2,1,0:T(8,128)(2,1)S(1)}, bf16[8,8,8,512]{3,2,1,0:T(8,128)(2,1)}, u32[]{:S(2)}, u32[]{:S(2)}) collective-permute-start(bf16[8,8,8,512]{3,2,1,0:T(8,128)(2,1)S(1)} %get-tuple-element.523), channel_id=1, source_target_pairs={{32,0},{64,32},{96,64},{128,96},{160,128},{192,160},{224,192},{33,... | collective-permute-start | bytes 1572872 | tf_op jit(solution)/shard_map/while/body/eval_jaxpr/ppermute | solution.py:29
  345.9 8.3 %collective-permute-start.3 = (bf16[8,8,4,512]{3,2,1,0:T(4,128)(2,1)}, bf16[8,8,4,512]{3,2,1,0:T(4,128)(2,1)}, u32[]{:S(2)}, u32[]{:S(2)}) collective-permute-start(bf16[8,8,4,512]{3,2,1,0:T(4,128)(2,1)} %get-tuple-element.439), channel_id=1, source_target_pairs={{1,0},{2,1},{3,2},{4,3},{5,4},{6,5},{7,6},{8,7},{9,8},{10,9},{11,1... | collective-permute-start | bytes 786440 | tf_op jit(solution)/shard_map/while/body/eval_jaxpr/ppermute | solution.py:19
  357.8 13.6 %collective-permute-start.5 = (bf16[8,8,8,512]{3,2,1,0:T(8,128)(2,1)S(1)}, bf16[8,8,8,512]{3,2,1,0:T(8,128)(2,1)}, u32[]{:S(2)}, u32[]{:S(2)}) collective-permute-start(bf16[8,8,8,512]{3,2,1,0:T(8,128)(2,1)S(1)} %get-tuple-element.523), channel_id=1, source_target_pairs={{32,0},{64,32},{96,64},{128,96},{160,128},{192,160},{224,192},{33,... | collective-permute-start | bytes 1572872 | tf_op jit(solution)/shard_map/while/body/eval_jaxpr/ppermute | solution.py:29
  374.9 8.3 %collective-permute-start.3 = (bf16[8,8,4,512]{3,2,1,0:T(4,128)(2,1)}, bf16[8,8,4,512]{3,2,1,0:T(4,128)(2,1)}, u32[]{:S(2)}, u32[]{:S(2)}) collective-permute-start(bf16[8,8,4,512]{3,2,1,0:T(4,128)(2,1)} %get-tuple-element.439), channel_id=1, source_target_pairs={{1,0},{2,1},{3,2},{4,3},{5,4},{6,5},{7,6},{8,7},{9,8},{10,9},{11,1... | collective-permute-start | bytes 786440 | tf_op jit(solution)/shard_map/while/body/eval_jaxpr/ppermute | solution.py:19
  386.7 11.5 %collective-permute-start.5 = (bf16[8,8,8,512]{3,2,1,0:T(8,128)(2,1)S(1)}, bf16[8,8,8,512]{3,2,1,0:T(8,128)(2,1)}, u32[]{:S(2)}, u32[]{:S(2)}) collective-permute-start(bf16[8,8,8,512]{3,2,1,0:T(8,128)(2,1)S(1)} %get-tuple-element.523), channel_id=1, source_target_pairs={{32,0},{64,32},{96,64},{128,96},{160,128},{192,160},{224,192},{33,... | collective-permute-start | bytes 1572872 | tf_op jit(solution)/shard_map/while/body/eval_jaxpr/ppermute | solution.py:29
  401.8 8.3 %collective-permute-start.3 = (bf16[8,8,4,512]{3,2,1,0:T(4,128)(2,1)}, bf16[8,8,4,512]{3,2,1,0:T(4,128)(2,1)}, u32[]{:S(2)}, u32[]{:S(2)}) collective-permute-start(bf16[8,8,4,512]{3,2,1,0:T(4,128)(2,1)} %get-tuple-element.439), channel_id=1, source_target_pairs={{1,0},{2,1},{3,2},{4,3},{5,4},{6,5},{7,6},{8,7},{9,8},{10,9},{11,1... | collective-permute-start | bytes 786440 | tf_op jit(solution)/shard_map/while/body/eval_jaxpr/ppermute | solution.py:19
  413.7 14.0 %collective-permute-start.5 = (bf16[8,8,8,512]{3,2,1,0:T(8,128)(2,1)S(1)}, bf16[8,8,8,512]{3,2,1,0:T(8,128)(2,1)}, u32[]{:S(2)}, u32[]{:S(2)}) collective-permute-start(bf16[8,8,8,512]{3,2,1,0:T(8,128)(2,1)S(1)} %get-tuple-element.523), channel_id=1, source_target_pairs={{32,0},{64,32},{96,64},{128,96},{160,128},{192,160},{224,192},{33,... | collective-permute-start | bytes 1572872 | tf_op jit(solution)/shard_map/while/body/eval_jaxpr/ppermute | solution.py:29
  431.3 8.3 %collective-permute-start.3 = (bf16[8,8,4,512]{3,2,1,0:T(4,128)(2,1)}, bf16[8,8,4,512]{3,2,1,0:T(4,128)(2,1)}, u32[]{:S(2)}, u32[]{:S(2)}) collective-permute-start(bf16[8,8,4,512]{3,2,1,0:T(4,128)(2,1)} %get-tuple-element.439), channel_id=1, source_target_pairs={{1,0},{2,1},{3,2},{4,3},{5,4},{6,5},{7,6},{8,7},{9,8},{10,9},{11,1... | collective-permute-start | bytes 786440 | tf_op jit(solution)/shard_map/while/body/eval_jaxpr/ppermute | solution.py:19
  443.1 56.5 %collective-permute-start.5 = (bf16[8,8,8,512]{3,2,1,0:T(8,128)(2,1)S(1)}, bf16[8,8,8,512]{3,2,1,0:T(8,128)(2,1)}, u32[]{:S(2)}, u32[]{:S(2)}) collective-permute-start(bf16[8,8,8,512]{3,2,1,0:T(8,128)(2,1)S(1)} %get-tuple-element.523), channel_id=1, source_target_pairs={{32,0},{64,32},{96,64},{128,96},{160,128},{192,160},{224,192},{33,... | collective-permute-start | bytes 1572872 | tf_op jit(solution)/shard_map/while/body/eval_jaxpr/ppermute | solution.py:29
  503.1 8.3 %collective-permute-start.3 = (bf16[8,8,4,512]{3,2,1,0:T(4,128)(2,1)}, bf16[8,8,4,512]{3,2,1,0:T(4,128)(2,1)}, u32[]{:S(2)}, u32[]{:S(2)}) collective-permute-start(bf16[8,8,4,512]{3,2,1,0:T(4,128)(2,1)} %get-tuple-element.439), channel_id=1, source_target_pairs={{1,0},{2,1},{3,2},{4,3},{5,4},{6,5},{7,6},{8,7},{9,8},{10,9},{11,1... | collective-permute-start | bytes 786440 | tf_op jit(solution)/shard_map/while/body/eval_jaxpr/ppermute | solution.py:19
  521.8 11.5 %collective-permute-start.5 = (bf16[8,8,8,512]{3,2,1,0:T(8,128)(2,1)S(1)}, bf16[8,8,8,512]{3,2,1,0:T(8,128)(2,1)}, u32[]{:S(2)}, u32[]{:S(2)}) collective-permute-start(bf16[8,8,8,512]{3,2,1,0:T(8,128)(2,1)S(1)} %get-tuple-element.523), channel_id=1, source_target_pairs={{32,0},{64,32},{96,64},{128,96},{160,128},{192,160},{224,192},{33,... | collective-permute-start | bytes 1572872 | tf_op jit(solution)/shard_map/while/body/eval_jaxpr/ppermute | solution.py:29
  536.8 8.3 %collective-permute-start.3 = (bf16[8,8,4,512]{3,2,1,0:T(4,128)(2,1)}, bf16[8,8,4,512]{3,2,1,0:T(4,128)(2,1)}, u32[]{:S(2)}, u32[]{:S(2)}) collective-permute-start(bf16[8,8,4,512]{3,2,1,0:T(4,128)(2,1)} %get-tuple-element.439), channel_id=1, source_target_pairs={{1,0},{2,1},{3,2},{4,3},{5,4},{6,5},{7,6},{8,7},{9,8},{10,9},{11,1... | collective-permute-start | bytes 786440 | tf_op jit(solution)/shard_map/while/body/eval_jaxpr/ppermute | solution.py:19
  555.5 10.0 %collective-permute-start.5 = (bf16[8,8,8,512]{3,2,1,0:T(8,128)(2,1)S(1)}, bf16[8,8,8,512]{3,2,1,0:T(8,128)(2,1)}, u32[]{:S(2)}, u32[]{:S(2)}) collective-permute-start(bf16[8,8,8,512]{3,2,1,0:T(8,128)(2,1)S(1)} %get-tuple-element.523), channel_id=1, source_target_pairs={{32,0},{64,32},{96,64},{128,96},{160,128},{192,160},{224,192},{33,... | collective-permute-start | bytes 1572872 | tf_op jit(solution)/shard_map/while/body/eval_jaxpr/ppermute | solution.py:29
  (15 other events, 995.1 us)
Sparse Core Ops, SparseCore 0:
  566.8 68.7 all-reduce.3
